TPU v7x, 128 devices: a whole 4x4x4 slice. The times are simulated.
128 devices in a mesh: row: 8 (over y_lo, z), col: 16 (over y_hi, x, core).
Axes of the slice: x: 4, y: 4 (y_hi: 2, y_lo: 2; y = y_hi * 2 + y_lo), z: 4, core: 2. Of those that a mesh axis runs over, the one named last changes fastest.
Arguments:
- features: bfloat16 [24576, 512], P(('col', 'row')), may hold values from -6 to 6
- out_grad: bfloat16 [24576, 512], P(('row', 'col')), may hold values from -6 to 6
- weight: bfloat16 [512, 512], replicated, may hold values from -0.25 to 0.25
- block_values: bfloat16 [8, 16, 288, 4096], P('row', 'col'), may hold values from -0.125 to 0.125
- block_coords: int32 [8, 16, 2, 288], P('row', 'col'), may hold values from 0 to 47, as said below
- block_counts: int32 [8, 16], P('row', 'col'), may hold values from 1 to 288, as said below
Outputs:
- activations: bfloat16 [24576, 512], P(('row', 'col'))
- weight_grad: float32 [512, 512], replicated
- feature_grad: bfloat16 [24576, 512], P(('col', 'row'))
Inputs may be any that keep to these rules, and one draw needn't show every extreme that they name: `block_coords`: entry 0 of a slot is a block row below 48, entry 1 a block column below 24; the 288 slots of a tile name distinct blocks. `block_counts`: slots from the count onward are padding: their coordinates and values are ignored. Some tile has exactly 288 live slots.
All inputs are finite; a program needn't handle non-finite values.
Results may differ from a plain program's by a relative error of at most 0.025.
Values may be sent and summed in bfloat16 or wider, within the bound.
No kernel may reach another device: no remote copies, remote signals or barrier semaphores. Data moves between devices by JAX's collectives and lax.ppermute only.
A program may use at most 128 MiB of HBM per device.

v0:
```python
import math
import jax
import jax.numpy as jnp
from jax import lax
from jax.sharding import PartitionSpec as P


def settle(term):
    return lax.optimization_barrier(term.astype(jnp.bfloat16)).astype(jnp.float32)


def per_device(features, out_grad, weight, block_values, block_coords, block_counts):
    row_devices = lax.axis_size("row")
    col_devices = lax.axis_size("col")
    node_count = features.shape[0]
    side = 64
    slot_total = block_values.shape[2]
    block_rows = node_count * col_devices // side
    block_cols = node_count * row_devices // side
    live_count = block_counts[0, 0]
    row_ids = block_coords[0, 0, 0]
    col_ids = block_coords[0, 0, 1]
    slot_vals = block_values.reshape(slot_total, side, side)
    live = jnp.arange(slot_total, dtype=jnp.int32) < live_count
    slot_vals = jnp.where(live[:, None, None], slot_vals, jnp.zeros_like(slot_vals))
    panel = lax.all_gather(features, "row", axis=0, tiled=True)
    dense_tile = jnp.zeros((block_rows, side, block_cols, side), jnp.bfloat16)
    dense_tile = dense_tile.at[row_ids, :, col_ids, :].add(slot_vals)
    dense_tile = dense_tile.reshape(block_rows * side, block_cols * side)
    partial_agg = settle(jnp.dot(dense_tile, panel, preferred_element_type=jnp.float32))
    aggregated = lax.psum_scatter(
        partial_agg.astype(jnp.bfloat16), "col", scatter_dimension=0, tiled=True
    )
    pre_act = jnp.dot(aggregated, weight, preferred_element_type=jnp.float32)
    sigmoid_pre = jax.nn.sigmoid(pre_act)
    activations = (pre_act * sigmoid_pre).astype(jnp.bfloat16)
    grad_pre = (
        out_grad.astype(jnp.float32) * sigmoid_pre * (1.0 + pre_act * (1.0 - sigmoid_pre))
    ).astype(jnp.bfloat16)
    activations, grad_pre = (activations, grad_pre)
    grad_agg = lax.dot_general(
        grad_pre, weight, (((1,), (1,)), ((), ())), preferred_element_type=jnp.float32
    ).astype(jnp.bfloat16)
    grad_rows = lax.all_gather(grad_agg, "col", axis=0, tiled=True)
    local_wgrad = lax.dot_general(
        aggregated, grad_pre, (((0,), (0,)), ((), ())), preferred_element_type=jnp.float32
    )
    total_nodes = node_count * row_devices * col_devices
    weight_grad = lax.psum(local_wgrad, ("row", "col")) * jnp.float32(1.0 / math.sqrt(total_nodes))
    partial_grad = settle(
        lax.dot_general(
            dense_tile, grad_rows, (((0,), (0,)), ((), ())), preferred_element_type=jnp.float32
        )
    )
    feature_grad = lax.psum_scatter(
        partial_grad.astype(jnp.bfloat16), "row", scatter_dimension=0, tiled=True
    )
    return (activations, weight_grad, feature_grad)


def solution(mesh):
    return jax.shard_map(
        per_device,
        mesh=mesh,
        in_specs=(
            P(("col", "row"), None),
            P(("row", "col"), None),
            P(),
            P("row", "col", None, None),
            P("row", "col", None, None),
            P("row", "col"),
        ),
        out_specs=(P(("row", "col"), None), P(), P(("col", "row"), None)),
        check_vma=False,
    )
```

profile of v0, /device:TPU:0, one launch (start us, length us, event | category | flops | bytes accessed | tf_op | source)
XLA Modules:
  0.0 468.9 jit_solution(1539356239016432633)
XLA Ops:
  7.2 0.0 copy-start
  7.2 0.0 all-gather.3.cloned.1.call-start
  7.2 0.7 all-gather.3.cloned.1.call-update
  7.9 0.0 reduce-scatter.3.cloned.1.call-start
  8.0 4.5 copy.9
  13.1 3.9 broadcast_select_fusion
  17.0 0.0 copy-start.1
  17.0 9.9 %copy.10 = bf16[288,64,64]{2,1,0:T(8,128)(2,1)} copy(bf16[288,64,64]{0,2,1:T(8,128)(2,1)} %broadcast_select_fusion) | data formatting | bytes 4718592 | tf_op jit(solution)/shard_map/jit(_where)/select_n | solution.py:25
  26.9 0.0 copy-done.1
  26.9 7.1 %broadcast_in_dim.17 = bf16[48,64,24,64]{3,1,2,0:T(8,128)(2,1)} broadcast(bf16[]{:T(256)} %constant.6.clone.1), dimensions={} | broadcast | bytes 9437186 | tf_op jit(solution)/shard_map/broadcast_in_dim | solution.py:27
  34.0 45.5 %scatter_fusion = bf16[48,64,24,64]{3,1,2,0:T(8,128)(2,1)} fusion(bf16[48,64,24,64]{3,1,2,0:T(8,128)(2,1)} %broadcast_in_dim.17, s32[288]{0:T(512)S(1)} %fusion.1, bf16[288,64,64]{2,1,0:T(8,128)(2,1)} %copy.10), kind=kCustom, calls=%fused_computation | custom fusion | flops 1179648 | bytes 7080192 | tf_op jit(solution)/shard_map/scatter-add | solution.py:28
  79.6 22.7 %copy.11 = bf16[48,64,24,64]{3,2,1,0:T(8,128)(2,1)} copy(bf16[48,64,24,64]{3,1,2,0:T(8,128)(2,1)} %scatter_fusion) | data formatting | bytes 18874368 | tf_op jit(solution)/shard_map/scatter-add | solution.py:28
  102.2 24.6 %reshape.73 = bf16[3072,1536]{1,0:T(8,128)(2,1)} reshape(bf16[48,64,24,64]{3,2,1,0:T(8,128)(2,1)} %copy.11) | data formatting | bytes 18874368 | tf_op jit(solution)/shard_map/reshape | solution.py:29
  126.8 0.0 all-gather.3.cloned.1.call-done
  126.8 9.2 %convolution_convert_fusion = bf16[3072,512]{1,0:T(8,128)(2,1)} fusion(bf16[3072,1536]{1,0:T(8,128)(2,1)} %reshape.73, bf16[1536,512]{1,0:T(8,128)(2,1)} %all-gather.3.cloned.1.call-done), kind=kOutput, calls=%fused_computation.1 | convolution fusion | flops 4833411072 | bytes 14155776 | tf_op jit(solution)/shard_map/dot_general | solution.py:30
  136.1 0.0 copy-start.2
  136.1 0.0 reduce-scatter.3.cloned.1.call-update
  136.1 0.0 all-gather.5.cloned.1.call-start
  136.1 77.8 %reduce-scatter.3.cloned.1.call-done = bf16[192,512]{1,0:T(8,128)(2,1)} async-done(((bf16[3072,512]{1,0:T(8,128)(2,1)}), bf16[192,512]{1,0:T(8,128)(2,1)}) %reduce-scatter.3.cloned.1.call-update) | async-done | bytes 196624 | tf_op jit(solution)/shard_map/reduce_scatter | solution.py:31
  213.9 0.0 copy-done
  213.9 0.0 copy-start.3
  213.9 2.0 multiply_convert_fusion.1
  216.0 0.0 copy-done.2
  216.0 1.0 convolution_convert_fusion.2
  217.0 0.0 all-gather.5.cloned.1.call-update
  217.0 0.0 all-reduce.2.cloned.1.call-start
  217.1 0.0 copy-done.3
  217.1 1.4 fusion.2
  218.5 0.0 all-reduce.2.cloned.1.call-update
  218.5 0.2 reduce-scatter.5.cloned.1.call-start
  218.7 49.6 %all-gather.5.cloned.1.call-done = bf16[3072,512]{1,0:T(8,128)(2,1)} async-done(((bf16[192,512]{1,0:T(8,128)(2,1)}), bf16[3072,512]{1,0:T(8,128)(2,1)}) %all-gather.5.cloned.1.call-update) | async-done | bytes 3145744 | tf_op jit(solution)/shard_map/all_gather | solution.py:44
  268.3 10.4 %convolution_convert_fusion.1 = bf16[1536,512]{1,0:T(8,128)(2,1)} fusion(bf16[3072,1536]{1,0:T(8,128)(2,1)} %reshape.73, bf16[3072,512]{1,0:T(8,128)(2,1)} %all-gather.5.cloned.1.call-done), kind=kOutput, calls=%fused_computation.3 | convolution fusion | flops 4832624640 | bytes 14155776 | tf_op jit(solution)/shard_map/dot_general | solution.py:51
  278.7 0.0 reduce-scatter.5.cloned.1.call-update
  278.7 140.3 %all-reduce.2.cloned.1.call-done = f32[512,512]{1,0:T(8,128)} async-done(((f32[512,512]{1,0:T(8,128)}), f32[512,512]{1,0:T(8,128)}) %all-reduce.2.cloned.1.call-update) | async-done | bytes 1048592 | tf_op jit(solution)/shard_map/psum | solution.py:49
  419.0 2.3 broadcast_multiply_fusion
  421.3 41.0 %reduce-scatter.5.cloned.1.call-done = bf16[192,512]{1,0:T(8,128)(2,1)} async-done(((bf16[1536,512]{1,0:T(8,128)(2,1)}), bf16[192,512]{1,0:T(8,128)(2,1)}) %reduce-scatter.5.cloned.1.call-update) | async-done | bytes 196624 | tf_op jit(solution)/shard_map/reduce_scatter | solution.py:55
  (2 shorter events, 0.0 us)
Async XLA Ops:
  7.2 206.8 %copy-start = (bf16[512,512]{1,0:T(8,128)(2,1)S(1)}, bf16[512,512]{1,0:T(8,128)(2,1)}, u32[]{:S(2)}) copy-start(bf16[512,512]{1,0:T(8,128)(2,1)} %param.8) | copy-start | bytes 1572868
  7.2 119.6 %all-gather.3.cloned.1.call-start = ((), (), s32[]{:S(2)}) async-start(), calls=%async_computation.2 | async-start | bytes 1769472 | tf_op jit(solution)/shard_map/all_gather | solution.py:26
  7.9 206.0 %reduce-scatter.3.cloned.1.call-start = ((), (), s32[]{:S(2)}) async-start(), calls=%async_computation.3 | async-start | bytes 3342336 | tf_op jit(solution)/shard_map/reduce_scatter | solution.py:31
  17.0 10.0 %copy-start.1 = (s32[1,1,2,288]{3,2,1,0:T(2,128)S(1)}, s32[1,1,2,288]{3,2,1,0:T(2,128)}, u32[]{:S(2)}) copy-start(s32[1,1,2,288]{3,2,1,0:T(2,128)} %param.10) | copy-start | bytes 6916
  136.1 79.9 %copy-start.2 = (bf16[192,512]{1,0:T(8,128)(2,1)S(1)}, bf16[192,512]{1,0:T(8,128)(2,1)}, u32[]{:S(2)}) copy-start(bf16[192,512]{1,0:T(8,128)(2,1)} %param.7) | copy-start | bytes 589828
  136.1 132.2 %all-gather.5.cloned.1.call-start = ((), (), s32[]{:S(2)}) async-start(), calls=%async_computation.5 | async-start | bytes 3342336 | tf_op jit(solution)/shard_map/all_gather | solution.py:44
  213.9 3.1 copy-start.3
  217.0 202.0 %all-reduce.2.cloned.1.call-start = ((), (), s32[]{:S(2)}) async-start(), calls=%async_computation.4 | async-start | bytes 2097152 | tf_op jit(solution)/shard_map/psum | solution.py:49
  218.5 243.9 %reduce-scatter.5.cloned.1.call-start = ((), (), s32[]{:S(2)}) async-start(), calls=%async_computation.6 | async-start | bytes 1769472 | tf_op jit(solution)/shard_map/reduce_scatter | solution.py:55
Sparse Core Ops, SparseCore 0:
  9.7 43.1 all-gather.2
  136.2 77.6 reduce-scatter.2
  217.1 51.1 all-gather.4
  273.5 145.4 all-reduce.1
  422.0 40.3 reduce-scatter.4
where the time goes:
time: 471 us; the launch traced here: 469 us
  waiting for transfers between devices  309 us (66%)
  local copies, waits for them, and re-layouts  68.8 us (15%)
  other arithmetic  51.7 us (11%)
  matrix products  24.1 us (5%)
  between operations  14.5 us (3%)
    psum x1, waiting for transfers between devices, per_device(): lax.psum(local_wgrad, ('row', 'col'))  140 us
    reduce_scatter x1, waiting for transfers between devices, per_device(): lax.psum_scatter(partial_agg.astype(jnp.bfloat16), 'col', scatter_dimensi...  77.8 us
    all_gather x1, waiting for transfers between devices, per_device(): grad_rows = lax.all_gather(grad_agg, 'col', axis=0, tiled=True)  49.6 us
    scatter-add x1, other arithmetic, per_device(): dense_tile = dense_tile.at[row_ids, :, col_ids, :].add(slot_vals)  45.5 us
    reduce_scatter x1, waiting for transfers between devices, per_device(): lax.psum_scatter(partial_grad.astype(jnp.bfloat16), 'row', scatter_dimens...  41 us
    reshape x1, local copies, waits for them, and re-layouts, per_device(): dense_tile = dense_tile.reshape(block_rows * side, block_cols * side)  24.6 us
    scatter-add x1, local copies, waits for them, and re-layouts, per_device(): dense_tile = dense_tile.at[row_ids, :, col_ids, :].add(slot_vals)  22.7 us
    dot_general x1, matrix products, per_device(): lax.dot_general(dense_tile, grad_rows, (((0,), (0,)), ((), ())), preferre...  10.4 us
  transfers between devices with their start and end apart: 5, of which 4 were waited for; matrix products, arithmetic and copies ran while one was open for 28% of the time, Pallas kernels for 0%

commit v1 on v0

--- a/solution.py
+++ b/solution.py
@@ -46,7 +46,9 @@
         aggregated, grad_pre, (((0,), (0,)), ((), ())), preferred_element_type=jnp.float32
     )
     total_nodes = node_count * row_devices * col_devices
-    weight_grad = lax.psum(local_wgrad, ("row", "col")) * jnp.float32(1.0 / math.sqrt(total_nodes))
+    weight_grad = lax.psum(lax.psum(local_wgrad, "row"), "col") * jnp.float32(
+        1.0 / math.sqrt(total_nodes)
+    )
     partial_grad = settle(
         lax.dot_general(
             dense_tile, grad_rows, (((0,), (0,)), ((), ())), preferred_element_type=jnp.float32

time: 471 us -> 544 us (1.15)
  waiting for transfers between devices: 309 us -> 382 us
    psum x1 -> x2, waiting for transfers between devices: 140 us -> 206 us  [the longest x1 131 us: per_device(): lax.psum(lax.psum(local_wgrad, 'row'), 'col')]
  transfers between devices with their start and end apart: 5 -> 6, of which waited for: 4 -> 5; matrix products, arithmetic and copies ran while one was open for 28% -> 24% of each run, Pallas kernels for 0% -> 0%
where the time goes in v1:
time: 544 us; the launch traced here: 543 us
  waiting for transfers between devices  382 us (70%)
  local copies, waits for them, and re-layouts  68.8 us (13%)
  other arithmetic  51.7 us (10%)
  matrix products  25 us (5%)
  between operations  14.8 us (3%)
    psum x1, waiting for transfers between devices, per_device(): lax.psum(lax.psum(local_wgrad, 'row'), 'col')  131 us
    reduce_scatter x1, waiting for transfers between devices, per_device(): lax.psum_scatter(partial_agg.astype(jnp.bfloat16), 'col', scatter_dimensi...  77.8 us
    psum x1, waiting for transfers between devices, per_device(): lax.psum(local_wgrad, 'row')  75.2 us
    all_gather x1, waiting for transfers between devices, per_device(): grad_rows = lax.all_gather(grad_agg, 'col', axis=0, tiled=True)  54.4 us
    scatter-add x1, other arithmetic, per_device(): dense_tile = dense_tile.at[row_ids, :, col_ids, :].add(slot_vals)  45.6 us
    reduce_scatter x1, waiting for transfers between devices, per_device(): lax.psum_scatter(partial_grad.astype(jnp.bfloat16), 'row', scatter_dimens...  42.8 us
    reshape x1, local copies, waits for them, and re-layouts, per_device(): dense_tile = dense_tile.reshape(block_rows * side, block_cols * side)  24.6 us
    scatter-add x1, local copies, waits for them, and re-layouts, per_device(): dense_tile = dense_tile.at[row_ids, :, col_ids, :].add(slot_vals)  22.7 us
  transfers between devices with their start and end apart: 6, of which 5 were waited for; matrix products, arithmetic and copies ran while one was open for 24% of the time, Pallas kernels for 0%

profile of v1, /device:TPU:0, one launch (start us, length us, event | category | flops | bytes accessed | tf_op | source)
XLA Modules:
  0.0 542.7 jit_solution(6265975618853517446)
XLA Ops:
  7.2 0.0 copy-start
  7.2 0.0 all-gather.3.cloned.1.call-start
  7.2 0.7 all-gather.3.cloned.1.call-update
  7.9 0.0 reduce-scatter.3.cloned.1.call-start
  8.0 4.5 copy.9
  13.1 3.8 broadcast_select_fusion
  17.0 0.0 copy-start.1
  17.0 9.9 %copy.10 = bf16[288,64,64]{2,1,0:T(8,128)(2,1)} copy(bf16[288,64,64]{0,2,1:T(8,128)(2,1)} %broadcast_select_fusion) | data formatting | bytes 4718592 | tf_op jit(solution)/shard_map/jit(_where)/select_n | solution.py:25
  26.9 0.0 copy-done.1
  26.9 7.0 %broadcast_in_dim.17 = bf16[48,64,24,64]{3,1,2,0:T(8,128)(2,1)} broadcast(bf16[]{:T(256)} %constant.6.clone.1), dimensions={} | broadcast | bytes 9437186 | tf_op jit(solution)/shard_map/broadcast_in_dim | solution.py:27
  33.9 45.6 %scatter_fusion = bf16[48,64,24,64]{3,1,2,0:T(8,128)(2,1)} fusion(bf16[48,64,24,64]{3,1,2,0:T(8,128)(2,1)} %broadcast_in_dim.17, s32[288]{0:T(512)S(1)} %fusion.1, bf16[288,64,64]{2,1,0:T(8,128)(2,1)} %copy.10), kind=kCustom, calls=%fused_computation | custom fusion | flops 1179648 | bytes 7080192 | tf_op jit(solution)/shard_map/scatter-add | solution.py:28
  79.5 22.7 %copy.11 = bf16[48,64,24,64]{3,2,1,0:T(8,128)(2,1)} copy(bf16[48,64,24,64]{3,1,2,0:T(8,128)(2,1)} %scatter_fusion) | data formatting | bytes 18874368 | tf_op jit(solution)/shard_map/scatter-add | solution.py:28
  102.2 24.6 %reshape.73 = bf16[3072,1536]{1,0:T(8,128)(2,1)} reshape(bf16[48,64,24,64]{3,2,1,0:T(8,128)(2,1)} %copy.11) | data formatting | bytes 18874368 | tf_op jit(solution)/shard_map/reshape | solution.py:29
  126.8 0.0 all-gather.3.cloned.1.call-done
  126.8 9.2 %convolution_convert_fusion = bf16[3072,512]{1,0:T(8,128)(2,1)} fusion(bf16[3072,1536]{1,0:T(8,128)(2,1)} %reshape.73, bf16[1536,512]{1,0:T(8,128)(2,1)} %all-gather.3.cloned.1.call-done), kind=kOutput, calls=%fused_computation.1 | convolution fusion | flops 4833411072 | bytes 14155776 | tf_op jit(solution)/shard_map/dot_general | solution.py:30
  136.0 0.0 copy-start.2
  136.0 0.0 reduce-scatter.3.cloned.1.call-update
  136.1 0.0 all-reduce.3.cloned.1.call-start
  136.1 77.8 %reduce-scatter.3.cloned.1.call-done = bf16[192,512]{1,0:T(8,128)(2,1)} async-done(((bf16[3072,512]{1,0:T(8,128)(2,1)}), bf16[192,512]{1,0:T(8,128)(2,1)}) %reduce-scatter.3.cloned.1.call-update) | async-done | bytes 196624 | tf_op jit(solution)/shard_map/reduce_scatter | solution.py:31
  213.9 0.0 copy-done
  213.9 1.9 multiply_convert_fusion.1
  215.8 0.0 copy-done.2
  215.8 2.3 fusion.2
  218.2 0.0 all-reduce.3.cloned.1.call-update
  218.2 0.0 all-gather.5.cloned.1.call-start
  218.2 1.0 convolution_convert_fusion.2
  219.3 0.0 all-gather.5.cloned.1.call-update
  219.3 0.0 all-reduce.5.cloned.1.call-start
  219.3 75.2 %all-reduce.3.cloned.1.call-done = f32[512,512]{1,0:T(8,128)} async-done(((f32[512,512]{1,0:T(8,128)}), f32[512,512]{1,0:T(8,128)}) %all-reduce.3.cloned.1.call-update) | async-done | bytes 1048592 | tf_op jit(solution)/shard_map/psum | solution.py:49
  294.6 0.0 all-reduce.5.cloned.1.call-update
  294.6 0.2 reduce-scatter.5.cloned.1.call-start
  294.8 54.4 %all-gather.5.cloned.1.call-done = bf16[3072,512]{1,0:T(8,128)(2,1)} async-done(((bf16[192,512]{1,0:T(8,128)(2,1)}), bf16[3072,512]{1,0:T(8,128)(2,1)}) %all-gather.5.cloned.1.call-update) | async-done | bytes 3145744 | tf_op jit(solution)/shard_map/all_gather | solution.py:44
  349.2 10.4 %convolution_convert_fusion.1 = bf16[1536,512]{1,0:T(8,128)(2,1)} fusion(bf16[3072,1536]{1,0:T(8,128)(2,1)} %reshape.73, bf16[3072,512]{1,0:T(8,128)(2,1)} %all-gather.5.cloned.1.call-done), kind=kOutput, calls=%fused_computation.3 | convolution fusion | flops 4832624640 | bytes 14155776 | tf_op jit(solution)/shard_map/dot_general | solution.py:53
  359.6 0.0 reduce-scatter.5.cloned.1.call-update
  359.7 131.0 %all-reduce.5.cloned.1.call-done = f32[512,512]{1,0:T(8,128)} async-done(((f32[512,512]{1,0:T(8,128)}), f32[512,512]{1,0:T(8,128)}) %all-reduce.5.cloned.1.call-update) | async-done | bytes 1048592 | tf_op jit(solution)/shard_map/psum | solution.py:49
  490.7 2.3 broadcast_multiply_fusion
  493.0 42.8 %reduce-scatter.5.cloned.1.call-done = bf16[192,512]{1,0:T(8,128)(2,1)} async-done(((bf16[1536,512]{1,0:T(8,128)(2,1)}), bf16[192,512]{1,0:T(8,128)(2,1)}) %reduce-scatter.5.cloned.1.call-update) | async-done | bytes 196624 | tf_op jit(solution)/shard_map/reduce_scatter | solution.py:57
  (2 shorter events, 0.0 us)
Async XLA Ops:
  7.2 206.7 %copy-start = (bf16[512,512]{1,0:T(8,128)(2,1)S(1)}, bf16[512,512]{1,0:T(8,128)(2,1)}, u32[]{:S(2)}) copy-start(bf16[512,512]{1,0:T(8,128)(2,1)} %param.8) | copy-start | bytes 1572868
  7.2 119.6 %all-gather.3.cloned.1.call-start = ((), (), s32[]{:S(2)}) async-start(), calls=%async_computation.2 | async-start | bytes 1769472 | tf_op jit(solution)/shard_map/all_gather | solution.py:26
  7.9 206.0 %reduce-scatter.3.cloned.1.call-start = ((), (), s32[]{:S(2)}) async-start(), calls=%async_computation.3 | async-start | bytes 3342336 | tf_op jit(solution)/shard_map/reduce_scatter | solution.py:31
  17.0 9.9 %copy-start.1 = (s32[1,1,2,288]{3,2,1,0:T(2,128)S(1)}, s32[1,1,2,288]{3,2,1,0:T(2,128)}, u32[]{:S(2)}) copy-start(s32[1,1,2,288]{3,2,1,0:T(2,128)} %param.10) | copy-start | bytes 6916
  136.0 79.8 %copy-start.2 = (bf16[192,512]{1,0:T(8,128)(2,1)S(1)}, bf16[192,512]{1,0:T(8,128)(2,1)}, u32[]{:S(2)}) copy-start(bf16[192,512]{1,0:T(8,128)(2,1)} %param.7) | copy-start | bytes 589828
  136.1 158.5 %all-reduce.3.cloned.1.call-start = ((), (), s32[]{:S(2)}) async-start(), calls=%async_computation.4 | async-start | bytes 2097152 | tf_op jit(solution)/shard_map/psum | solution.py:49
  218.2 131.0 %all-gather.5.cloned.1.call-start = ((), (), s32[]{:S(2)}) async-start(), calls=%async_computation.6 | async-start | bytes 3342336 | tf_op jit(solution)/shard_map/all_gather | solution.py:44
  219.3 271.4 %all-reduce.5.cloned.1.call-start = ((), (), s32[]{:S(2)}) async-start(), calls=%async_computation.5 | async-start | bytes 2097152 | tf_op jit(solution)/shard_map/psum | solution.py:49
  294.6 241.2 %reduce-scatter.5.cloned.1.call-start = ((), (), s32[]{:S(2)}) async-start(), calls=%async_computation.7 | async-start | bytes 1769472 | tf_op jit(solution)/shard_map/reduce_scatter | solution.py:57
Sparse Core Ops, SparseCore 0:
  9.7 43.1 all-gather.2
  136.2 77.6 reduce-scatter.2
  218.3 76.2 all-reduce.2
  297.4 51.7 all-gather.4
  351.5 139.1 all-reduce.4
  493.7 42.1 reduce-scatter.4
